TPU v7x, 256 devices: a whole 4x4x8 slice. The times are simulated.
256 devices in a mesh: col: 32 (over z, x), row: 8 (over y, core).
Axes of the slice: x: 4, y: 4, z: 8, core: 2. Of those that a mesh axis runs over, the one named last changes fastest.
Arguments:
- trailing: float32 [24576, 16384], P('row', 'col'), may hold values from -6 to 6
- panel_rows: float32 [24576, 512], P(('row', 'col')), may hold values from -6 to 6
- pivot_block: float32 [512, 512], P('col'), as said below
- panel_fill: int32 [96, 2], replicated, may hold values 0 or 1
Outputs:
- updated: float32 [24576, 16384], P('row', 'col')
- panel_factor: float32 [24576, 512], P(('row', 'col'))
Inputs may be any that keep to these rules, and one draw needn't show every extreme that they name: `pivot_block`: Symmetric; each diagonal entry exceeds the sum of the magnitudes of the other entries of its row by at least 1. `panel_fill`: each entry is 1 with probability 0.15, independently of the others.
All inputs are finite; a program needn't handle non-finite values.
Results may differ from a plain program's by a relative error of at most 0.00008.
Values sent between devices are 32-bit elements; how exact they have to be, the bound alone decides.
A program may use at most 128 MiB of HBM per device.

v0:
```python
import jax
import jax.numpy as jnp
from jax import lax
from jax.sharding import PartitionSpec as P


def from_root(value, axis, source):
    kept = jnp.where(lax.axis_index(axis) == source, value, 0).astype(value.dtype)
    return lax.psum(kept, axis)


def apply_fill(values, row_start, fill_table, block_size):
    row_count = values.shape[0]
    blocks = (row_start + jnp.arange(row_count, dtype=jnp.int32)) // block_size
    one_hot = (blocks[:, None] == jnp.arange(fill_table.shape[0], dtype=jnp.int32)[None, :]).astype(
        jnp.float32
    )
    flags = jnp.dot(one_hot, fill_table.astype(jnp.float32), precision=lax.Precision.HIGHEST)
    shaped = values.reshape(row_count, 2, block_size) * flags[:, :, None]
    return shaped.reshape(row_count, 2 * block_size)


def solve_rows(values, factor):
    return lax.linalg.triangular_solve(
        factor, values, left_side=False, lower=True, transpose_a=True
    )


def per_device(trailing, panel_rows, pivot_block, panel_fill):
    block_size = panel_rows.shape[1] // 2
    piece_rows = panel_rows.shape[0]
    col_count = lax.axis_size("col")
    col_index = lax.axis_index("col")
    row_index = lax.axis_index("row")
    local_rows = piece_rows * col_count
    slab_start = row_index * local_rows
    pivot_full = lax.all_gather(pivot_block, "col", axis=0, tiled=True)
    factor = jnp.linalg.cholesky(pivot_full)
    piece_start = slab_start + col_index * piece_rows
    own_factor = solve_rows(apply_fill(panel_rows, piece_start, panel_fill, block_size), factor)
    row_side = lax.all_gather(own_factor, "col", axis=0, tiled=True)
    column_count = trailing.shape[1]
    column_start = col_index * column_count
    owner_row = column_start // local_rows
    offered = lax.dynamic_slice_in_dim(row_side, column_start - slab_start, column_count, 0)
    column_side = from_root(offered, "row", owner_row)
    update = lax.dot_general(
        row_side,
        column_side,
        (((1,), (1,)), ((), ())),
        precision=lax.Precision.HIGHEST,
        preferred_element_type=jnp.float32,
    )
    return (trailing - update, own_factor)


def solution(mesh):
    in_specs = (P("row", "col"), P(("row", "col"), None), P("col", None), P())
    out_specs = (P("row", "col"), P(("row", "col"), None))
    return jax.shard_map(
        per_device, mesh=mesh, in_specs=in_specs, out_specs=out_specs, check_vma=False
    )
```

profile of v0, /device:TPU:2, one launch (start us, length us, event | category | flops | bytes accessed | tf_op | source)
XLA Modules:
  0.0 402.2 jit_solution(7585898141999107908)
XLA Ops:
  8.0 0.9 fusion.28
  9.1 1.0 mul.24
  10.0 78.7 %all-gather.3.cloned.1.call-done = f32[512,512]{1,0:T(8,128)} async-done(((f32[16,512]{1,0:T(8,128)}), f32[512,512]{1,0:T(8,128)}) %all-gather.3.cloned.1.call-update) | async-done | bytes 1048592 | tf_op jit(solution)/shard_map/all_gather | solution.py:37
  88.7 1.6 copy.10
  90.3 1.4 fusion
  91.8 11.7 %cholesky.104 = f32[128,128]{1,0:T(8,128)S(1)} custom-call(f32[128,128]{1,0:T(8,128)S(1)} %cholesky.266), custom_call_target="Cholesky" | custom-call | tf_op jit(solution)/shard_map/jit(cholesky)/cholesky | solution.py:38
  103.5 9.8 %custom-call.30 = f32[1,128,128]{1,2,0:T(8,128)S(1)} custom-call(f32[1,128,128]{2,1,0:T(8,128)S(1)} %get-tuple-element.29), custom_call_target="InvertDiagBlocksLowerTriangular" | custom-call | tf_op jit(solution)/shard_map/jit(cholesky)/cholesky | solution.py:38
  114.1 11.7 %cholesky.217 = f32[128,128]{1,0:T(8,128)S(1)} custom-call(f32[128,128]{1,0:T(8,128)S(1)} %cholesky.270), custom_call_target="Cholesky" | custom-call | tf_op jit(solution)/shard_map/jit(cholesky)/cholesky | solution.py:38
  125.9 10.0 %custom-call.31 = f32[1,128,128]{1,2,0:T(8,128)S(1)} custom-call(f32[1,128,128]{2,1,0:T(8,128)S(1)} %get-tuple-element.26), custom_call_target="InvertDiagBlocksLowerTriangular" | custom-call | tf_op jit(solution)/shard_map/jit(cholesky)/cholesky | solution.py:38
  136.5 11.7 %cholesky.238 = f32[128,128]{1,0:T(8,128)S(1)} custom-call(f32[128,128]{1,0:T(8,128)S(1)} %cholesky.275), custom_call_target="Cholesky" | custom-call | tf_op jit(solution)/shard_map/jit(cholesky)/cholesky | solution.py:38
  148.3 0.7 compare_reduce_fusion.1
  149.0 9.8 %custom-call.32 = f32[1,128,128]{1,2,0:T(8,128)S(1)} custom-call(f32[1,128,128]{2,1,0:T(8,128)S(1)} %get-tuple-element.23), custom_call_target="InvertDiagBlocksLowerTriangular" | custom-call | tf_op jit(solution)/shard_map/jit(cholesky)/cholesky | solution.py:38
  159.4 11.9 %cholesky.255 = f32[128,128]{1,0:T(8,128)S(1)} custom-call(f32[128,128]{1,0:T(8,128)S(1)} %convolution_subtract_fusion.3), custom_call_target="Cholesky" | custom-call | tf_op jit(solution)/shard_map/jit(cholesky)/cholesky | solution.py:38
  175.3 8.5 %while.1 = (s32[]{:T(128)}, f32[512,512]{1,0:T(8,128)S(1)}, s32[4,2]{0,1:T(2,128)S(1)}, f32[4,128,128]{2,1,0:T(8,128)S(1)}, s32[]{:T(128)}) while((s32[]{:T(128)}, f32[512,512]{1,0:T(8,128)S(1)}, s32[4,2]{0,1:T(2,128)S(1)}, f32[4,128,128]{2,1,0:T(8,128)S(1)}, s32[]{:T(128)}) %tuple.31), condition=%wide.while_cond, body=%wide.while_body.sunk | while | flops 2 | bytes 131189 | solution.py:24
  176.0 1.4 bitcast_dynamic-update-slice_fusion.2
  178.1 1.4 bitcast_dynamic-update-slice_fusion.2
  180.2 1.4 bitcast_dynamic-update-slice_fusion.2
  182.3 1.4 bitcast_dynamic-update-slice_fusion.2
  183.8 39.3 %custom-call.33 = f32[4,128,128]{1,2,0:T(8,128)S(1)} custom-call(f32[4,128,128]{2,1,0:T(8,128)S(1)} %get-tuple-element.9), custom_call_target="InvertDiagBlocksLowerTriangular" | custom-call | tf_op jit(solution)/shard_map/triangular_solve | solution.py:24
  224.8 0.7 pad_maximum_fusion
  225.6 86.1 %all-gather.5.cloned.1.call-done = f32[3072,512]{1,0:T(8,128)} async-done(((f32[96,512]{1,0:T(8,128)}), f32[3072,512]{1,0:T(8,128)}) %all-gather.5.cloned.1.call-update) | async-done | bytes 6291472 | tf_op jit(solution)/shard_map/all_gather | solution.py:41
  311.8 2.3 dynamic-slice_select_fusion
  314.1 66.5 %all-reduce.3.cloned.1.call-done = f32[512,512]{1,0:T(8,128)} async-done(((f32[512,512]{1,0:T(8,128)}), f32[512,512]{1,0:T(8,128)}) %all-reduce.3.cloned.1.call-update) | async-done | bytes 1048592 | tf_op jit(solution)/shard_map/psum | solution.py:9
  380.5 15.1 %convolution_subtract_fusion = f32[3072,512]{1,0:T(8,128)} fusion(f32[3072,512]{1,0:T(8,128)} %param.4, f32[3072,512]{1,0:T(8,128)} %all-gather.5.cloned.1.call-done, f32[512,512]{1,0:T(8,128)} %all-reduce.3.cloned.1.call-done), kind=kOutput, calls=%fused_computation.2 | convolution fusion | flops 9665249280 | bytes 19922944 | tf_op jit(solution)/shard_map/dot_general | solution.py:47
  (44 shorter events, 9.0 us)
Async XLA Ops:
  7.2 81.6 %all-gather.3.cloned.1.call-start = ((), (), s32[]{:S(2)}) async-start(), calls=%async_computation | async-start | bytes 1081344 | tf_op jit(solution)/shard_map/all_gather | solution.py:37
  7.9 303.9 %all-gather.5.cloned.1.call-start = ((), (), s32[]{:S(2)}) async-start(), calls=%async_computation.1 | async-start | bytes 6488064 | tf_op jit(solution)/shard_map/all_gather | solution.py:41
  225.5 155.0 %all-reduce.3.cloned.1.call-start = ((), (), s32[]{:S(2)}) async-start(), calls=%async_computation.2 | async-start | bytes 2097152 | tf_op jit(solution)/shard_map/psum | solution.py:9
Sparse Core Ops, SparseCore 0:
  10.6 78.1 all-gather.2
  225.7 86.0 all-gather.4
  314.7 65.7 all-reduce.2
where the time goes:
time: 403 us; the launch traced here: 402 us
  waiting for transfers between devices  232 us (58%)
  other arithmetic  124 us (31%)
  matrix products  19.6 us (5%)
  between operations  16.6 us (4%)
  local copies, waits for them, and re-layouts  10.3 us (3%)
    all_gather x1, waiting for transfers between devices, per_device(): row_side = lax.all_gather(own_factor, 'col', axis=0, tiled=True)  86.1 us
    another operation x14, other arithmetic, per_device(): factor = jnp.linalg.cholesky(pivot_full)  78.7 us
    all_gather x1, waiting for transfers between devices, per_device(): pivot_full = lax.all_gather(pivot_block, 'col', axis=0, tiled=True)  78.7 us
    psum x1, waiting for transfers between devices, from_root(): return lax.psum(kept, axis)  66.5 us
    another operation x4, other arithmetic, solve_rows(): lax.linalg.triangular_solve(factor, values, left_side=False, lower=True,...  40.1 us
    dot_general x1, matrix products, per_device(): lax.dot_general(row_side, column_side, (((1,), (1,)), ((), ())), precisio...  15.1 us
    another operation x12, local copies, waits for them, and re-layouts  8.39 us
  transfers between devices with their start and end apart: 3, of which 3 were waited for; matrix products, arithmetic and copies ran while one was open for 1% of the time, Pallas kernels for 0%

commit v1 on v0

--- a/solution.py
+++ b/solution.py
@@ -34,7 +34,9 @@
     row_index = lax.axis_index("row")
     local_rows = piece_rows * col_count
     slab_start = row_index * local_rows
-    pivot_full = lax.all_gather(pivot_block, "col", axis=0, tiled=True)
+    pivot_full = jnp.concatenate(
+        lax.all_to_all(jnp.stack([pivot_block] * lax.axis_size("col")), "col", 0, 0), axis=0
+    )
     factor = jnp.linalg.cholesky(pivot_full)
     piece_start = slab_start + col_index * piece_rows
     own_factor = solve_rows(apply_fill(panel_rows, piece_start, panel_fill, block_size), factor)

time: 403 us -> 362 us (0.90)
  waiting for transfers between devices: 232 us -> 177 us
  starting transfers between devices: 0.12 us -> 11.7 us
    all_gather x1 -> x0, waiting for transfers between devices: 78.7 us -> none  [per_device(): pivot_full = lax.all_gather(pivot_block, 'col', axis=0, tiled=True)]
    all_to_all x0 -> x1, waiting for transfers between devices: none -> 25.9 us  [per_device(): lax.all_to_all(jnp.stack([pivot_block] * lax.axis_size('col')), 'col', 0, 0)]
    all_to_all x0 -> x1, starting transfers between devices: none -> 11.6 us  [per_device(): lax.all_to_all(jnp.stack([pivot_block] * lax.axis_size('col')), 'col', 0, 0)]
    another operation x12 -> x13, local copies, waits for them, and re-layouts: 8.39 us -> 12.4 us
where the time goes in v1:
time: 362 us; the launch traced here: 361 us
  waiting for transfers between devices  177 us (49%)
  other arithmetic  123 us (34%)
  matrix products  19.6 us (5%)
  between operations  16.8 us (5%)
  local copies, waits for them, and re-layouts  13 us (4%)
  starting transfers between devices  11.7 us (3%)
    all_gather x1, waiting for transfers between devices, per_device(): row_side = lax.all_gather(own_factor, 'col', axis=0, tiled=True)  84.4 us
    another operation x14, other arithmetic, per_device(): factor = jnp.linalg.cholesky(pivot_full)  78.8 us
    psum x1, waiting for transfers between devices, from_root(): return lax.psum(kept, axis)  66.5 us
    another operation x4, other arithmetic, solve_rows(): lax.linalg.triangular_solve(factor, values, left_side=False, lower=True,...  40.9 us
    all_to_all x1, waiting for transfers between devices, per_device(): lax.all_to_all(jnp.stack([pivot_block] * lax.axis_size('col')), 'col', 0, 0)  25.9 us
    dot_general x1, matrix products, per_device(): lax.dot_general(row_side, column_side, (((1,), (1,)), ((), ())), precisio...  15.1 us
    all_to_all x1, starting transfers between devices, per_device(): lax.all_to_all(jnp.stack([pivot_block] * lax.axis_size('col')), 'col', 0, 0)  11.6 us
    another operation x12, local copies, waits for them, and re-layouts  10.5 us
  transfers between devices with their start and end apart: 3, of which 3 were waited for; matrix products, arithmetic and copies ran while one was open for 1% of the time, Pallas kernels for 0%

profile of v1, /device:TPU:2, one launch (start us, length us, event | category | flops | bytes accessed | tf_op | source)
XLA Modules:
  0.0 361.1 jit_solution(8854732701757599269)
XLA Ops:
  7.2 1.9 stack.2
  9.0 11.6 %all-to-all-start = ((f32[32,16,512]{2,1,0:T(8,128)}), f32[32,16,512]{2,1,0:T(8,128)S(1)}, u32[]{:S(2)}, u32[]{:S(2)}) async-start(f32[32,16,512]{2,1,0:T(8,128)} %stack.2), calls=%async_computation | async-start | bytes 2097152 | tf_op jit(solution)/shard_map/all_to_all | solution.py:38
  20.7 0.9 fusion.28
  21.8 1.0 mul.24
  22.8 25.9 %all-to-all-done = f32[32,16,512]{2,1,0:T(8,128)S(1)} async-done(((f32[32,16,512]{2,1,0:T(8,128)}), f32[32,16,512]{2,1,0:T(8,128)S(1)}, u32[]{:S(2)}, u32[]{:S(2)}) %all-to-all-start) | async-done | bytes 1048608 | tf_op jit(solution)/shard_map/all_to_all | solution.py:38
  49.3 11.7 %cholesky.104 = f32[128,128]{1,0:T(8,128)S(1)} custom-call(f32[128,128]{1,0:T(8,128)S(1)} %cholesky.266), custom_call_target="Cholesky" | custom-call | tf_op jit(solution)/shard_map/jit(cholesky)/cholesky | solution.py:40
  61.1 9.8 %custom-call.30 = f32[1,128,128]{1,2,0:T(8,128)S(1)} custom-call(f32[1,128,128]{2,1,0:T(8,128)S(1)} %get-tuple-element.29), custom_call_target="InvertDiagBlocksLowerTriangular" | custom-call | tf_op jit(solution)/shard_map/jit(cholesky)/cholesky | solution.py:40
  71.7 11.7 %cholesky.217 = f32[128,128]{1,0:T(8,128)S(1)} custom-call(f32[128,128]{1,0:T(8,128)S(1)} %cholesky.270), custom_call_target="Cholesky" | custom-call | tf_op jit(solution)/shard_map/jit(cholesky)/cholesky | solution.py:40
  83.4 9.9 %custom-call.31 = f32[1,128,128]{1,2,0:T(8,128)S(1)} custom-call(f32[1,128,128]{2,1,0:T(8,128)S(1)} %get-tuple-element.26), custom_call_target="InvertDiagBlocksLowerTriangular" | custom-call | tf_op jit(solution)/shard_map/jit(cholesky)/cholesky | solution.py:40
  94.0 11.7 %cholesky.238 = f32[128,128]{1,0:T(8,128)S(1)} custom-call(f32[128,128]{1,0:T(8,128)S(1)} %cholesky.275), custom_call_target="Cholesky" | custom-call | tf_op jit(solution)/shard_map/jit(cholesky)/cholesky | solution.py:40
  105.8 0.7 compare_reduce_fusion.1
  106.5 9.8 %custom-call.32 = f32[1,128,128]{1,2,0:T(8,128)S(1)} custom-call(f32[1,128,128]{2,1,0:T(8,128)S(1)} %get-tuple-element.23), custom_call_target="InvertDiagBlocksLowerTriangular" | custom-call | tf_op jit(solution)/shard_map/jit(cholesky)/cholesky | solution.py:40
  116.9 11.7 %cholesky.255 = f32[128,128]{1,0:T(8,128)S(1)} custom-call(f32[128,128]{1,0:T(8,128)S(1)} %convolution_subtract_fusion.3), custom_call_target="Cholesky" | custom-call | tf_op jit(solution)/shard_map/jit(cholesky)/cholesky | solution.py:40
  132.8 10.5 %while.1 = (s32[]{:T(128)}, f32[512,512]{1,0:T(8,128)S(1)}, s32[4,2]{0,1:T(2,128)S(1)}, f32[4,128,128]{2,1,0:T(8,128)}, s32[]{:T(128)}) while((s32[]{:T(128)}, f32[512,512]{1,0:T(8,128)S(1)}, s32[4,2]{0,1:T(2,128)S(1)}, f32[4,128,128]{2,1,0:T(8,128)}, s32[]{:T(128)}) %tuple.31), condition=%wide.while_cond, body=%wide.while_body.sunk | while | flops 2 | bytes 132205 | solution.py:24
  133.4 2.0 bitcast_dynamic-update-slice_fusion.2
  136.1 2.0 bitcast_dynamic-update-slice_fusion.2
  138.7 2.0 bitcast_dynamic-update-slice_fusion.2
  141.3 2.0 bitcast_dynamic-update-slice_fusion.2
  143.3 40.1 %custom-call.33 = f32[4,128,128]{1,2,0:T(8,128)S(1)} custom-call(f32[4,128,128]{2,1,0:T(8,128)} %get-tuple-element.9), custom_call_target="InvertDiagBlocksLowerTriangular" | custom-call | tf_op jit(solution)/shard_map/triangular_solve | solution.py:24
  185.2 0.7 pad_maximum_fusion
  186.0 84.4 %all-gather.2.cloned.1.call-done = f32[3072,512]{1,0:T(8,128)} async-done(((f32[96,512]{1,0:T(8,128)}), f32[3072,512]{1,0:T(8,128)}) %all-gather.2.cloned.1.call-update) | async-done | bytes 6291472 | tf_op jit(solution)/shard_map/all_gather | solution.py:43
  270.4 2.3 dynamic-slice_select_fusion
  272.7 66.5 %all-reduce.3.cloned.1.call-done = f32[512,512]{1,0:T(8,128)} async-done(((f32[512,512]{1,0:T(8,128)}), f32[512,512]{1,0:T(8,128)}) %all-reduce.3.cloned.1.call-update) | async-done | bytes 1048592 | tf_op jit(solution)/shard_map/psum | solution.py:9
  339.2 15.1 %convolution_subtract_fusion = f32[3072,512]{1,0:T(8,128)} fusion(f32[3072,512]{1,0:T(8,128)} %param.4, f32[3072,512]{1,0:T(8,128)} %all-gather.2.cloned.1.call-done, f32[512,512]{1,0:T(8,128)} %all-reduce.3.cloned.1.call-done), kind=kOutput, calls=%fused_computation.2 | convolution fusion | flops 9665249280 | bytes 19922944 | tf_op jit(solution)/shard_map/dot_general | solution.py:49
  (44 shorter events, 9.0 us)
Async XLA Ops:
  9.0 39.7 %all-to-all-start = ((f32[32,16,512]{2,1,0:T(8,128)}), f32[32,16,512]{2,1,0:T(8,128)S(1)}, u32[]{:S(2)}, u32[]{:S(2)}) async-start(f32[32,16,512]{2,1,0:T(8,128)} %stack.2), calls=%async_computation | async-start | bytes 2097152 | tf_op jit(solution)/shard_map/all_to_all | solution.py:38
  20.6 249.8 %all-gather.2.cloned.1.call-start = ((), (), s32[]{:S(2)}) async-start(), calls=%async_computation.1 | async-start | bytes 6488064 | tf_op jit(solution)/shard_map/all_gather | solution.py:43
  185.9 153.3 %all-reduce.3.cloned.1.call-start = ((), (), s32[]{:S(2)}) async-start(), calls=%async_computation.2 | async-start | bytes 2097152 | tf_op jit(solution)/shard_map/psum | solution.py:9
Sparse Core Ops, SparseCore 0:
  186.0 84.3 all-gather.1
  273.3 65.7 all-reduce.2

commit v2 on v0

--- a/solution.py
+++ b/solution.py
@@ -6,7 +6,7 @@
 
 def from_root(value, axis, source):
     kept = jnp.where(lax.axis_index(axis) == source, value, 0).astype(value.dtype)
-    return lax.psum(kept, axis)
+    return jnp.sum(lax.all_gather(kept, axis), axis=0)
 
 
 def apply_fill(values, row_start, fill_table, block_size):

time: 403 us -> 392 us (0.973)
  waiting for transfers between devices: 232 us -> 216 us
    psum x1 -> x0, waiting for transfers between devices: 66.5 us -> none  [from_root(): return lax.psum(kept, axis)]
    all_gather x0 -> x1, waiting for transfers between devices: none -> 50.7 us  [from_root(): return jnp.sum(lax.all_gather(kept, axis), axis=0)]
    reduce_sum x0 -> x1, other arithmetic: none -> 4.49 us  [from_root(): return jnp.sum(lax.all_gather(kept, axis), axis=0)]
where the time goes in v2:
time: 392 us; the launch traced here: 391 us
  waiting for transfers between devices  216 us (55%)
  other arithmetic  128 us (33%)
  matrix products  19.4 us (5%)
  between operations  16.6 us (4%)
  local copies, waits for them, and re-layouts  10.3 us (3%)
    all_gather x1, waiting for transfers between devices, per_device(): row_side = lax.all_gather(own_factor, 'col', axis=0, tiled=True)  86.1 us
    another operation x14, other arithmetic, per_device(): factor = jnp.linalg.cholesky(pivot_full)  78.7 us
    all_gather x1, waiting for transfers between devices, per_device(): pivot_full = lax.all_gather(pivot_block, 'col', axis=0, tiled=True)  78.7 us
    all_gather x1, waiting for transfers between devices, from_root(): return jnp.sum(lax.all_gather(kept, axis), axis=0)  50.7 us
    another operation x4, other arithmetic, solve_rows(): lax.linalg.triangular_solve(factor, values, left_side=False, lower=True,...  40.1 us
    dot_general x1, matrix products, per_device(): lax.dot_general(row_side, column_side, (((1,), (1,)), ((), ())), precisio...  14.9 us
    another operation x12, local copies, waits for them, and re-layouts  8.39 us
  transfers between devices with their start and end apart: 3, of which 3 were waited for; matrix products, arithmetic and copies ran while one was open for 1% of the time, Pallas kernels for 0%

profile of v2, /device:TPU:2, one launch (start us, length us, event | category | flops | bytes accessed | tf_op | source)
XLA Modules:
  0.0 390.7 jit_solution(17263039285143425229)
XLA Ops:
  8.0 0.9 fusion.28
  9.1 1.0 mul.24
  10.0 78.7 %all-gather.5.cloned.1.call-done = f32[512,512]{1,0:T(8,128)} async-done(((f32[16,512]{1,0:T(8,128)}), f32[512,512]{1,0:T(8,128)}) %all-gather.5.cloned.1.call-update) | async-done | bytes 1048592 | tf_op jit(solution)/shard_map/all_gather | solution.py:37
  88.7 1.6 copy.10
  90.3 1.4 fusion
  91.8 11.7 %cholesky.104 = f32[128,128]{1,0:T(8,128)S(1)} custom-call(f32[128,128]{1,0:T(8,128)S(1)} %cholesky.266), custom_call_target="Cholesky" | custom-call | tf_op jit(solution)/shard_map/jit(cholesky)/cholesky | solution.py:38
  103.5 9.8 %custom-call.30 = f32[1,128,128]{1,2,0:T(8,128)S(1)} custom-call(f32[1,128,128]{2,1,0:T(8,128)S(1)} %get-tuple-element.29), custom_call_target="InvertDiagBlocksLowerTriangular" | custom-call | tf_op jit(solution)/shard_map/jit(cholesky)/cholesky | solution.py:38
  114.1 11.7 %cholesky.217 = f32[128,128]{1,0:T(8,128)S(1)} custom-call(f32[128,128]{1,0:T(8,128)S(1)} %cholesky.270), custom_call_target="Cholesky" | custom-call | tf_op jit(solution)/shard_map/jit(cholesky)/cholesky | solution.py:38
  125.9 10.0 %custom-call.31 = f32[1,128,128]{1,2,0:T(8,128)S(1)} custom-call(f32[1,128,128]{2,1,0:T(8,128)S(1)} %get-tuple-element.26), custom_call_target="InvertDiagBlocksLowerTriangular" | custom-call | tf_op jit(solution)/shard_map/jit(cholesky)/cholesky | solution.py:38
  136.5 11.7 %cholesky.238 = f32[128,128]{1,0:T(8,128)S(1)} custom-call(f32[128,128]{1,0:T(8,128)S(1)} %cholesky.275), custom_call_target="Cholesky" | custom-call | tf_op jit(solution)/shard_map/jit(cholesky)/cholesky | solution.py:38
  148.3 0.7 compare_reduce_fusion.1
  149.0 9.8 %custom-call.32 = f32[1,128,128]{1,2,0:T(8,128)S(1)} custom-call(f32[1,128,128]{2,1,0:T(8,128)S(1)} %get-tuple-element.23), custom_call_target="InvertDiagBlocksLowerTriangular" | custom-call | tf_op jit(solution)/shard_map/jit(cholesky)/cholesky | solution.py:38
  159.4 11.9 %cholesky.255 = f32[128,128]{1,0:T(8,128)S(1)} custom-call(f32[128,128]{1,0:T(8,128)S(1)} %convolution_subtract_fusion.3), custom_call_target="Cholesky" | custom-call | tf_op jit(solution)/shard_map/jit(cholesky)/cholesky | solution.py:38
  175.3 8.5 %while.1 = (s32[]{:T(128)}, f32[512,512]{1,0:T(8,128)S(1)}, s32[4,2]{0,1:T(2,128)S(1)}, f32[4,128,128]{2,1,0:T(8,128)S(1)}, s32[]{:T(128)}) while((s32[]{:T(128)}, f32[512,512]{1,0:T(8,128)S(1)}, s32[4,2]{0,1:T(2,128)S(1)}, f32[4,128,128]{2,1,0:T(8,128)S(1)}, s32[]{:T(128)}) %tuple.31), condition=%wide.while_cond, body=%wide.while_body.sunk | while | flops 2 | bytes 131189 | solution.py:24
  176.0 1.4 bitcast_dynamic-update-slice_fusion.2
  178.1 1.4 bitcast_dynamic-update-slice_fusion.2
  180.2 1.4 bitcast_dynamic-update-slice_fusion.2
  182.3 1.4 bitcast_dynamic-update-slice_fusion.2
  183.8 39.3 %custom-call.33 = f32[4,128,128]{1,2,0:T(8,128)S(1)} custom-call(f32[4,128,128]{2,1,0:T(8,128)S(1)} %get-tuple-element.9), custom_call_target="InvertDiagBlocksLowerTriangular" | custom-call | tf_op jit(solution)/shard_map/triangular_solve | solution.py:24
  225.6 86.1 %all-gather.7.cloned.1.call-done = f32[3072,512]{1,0:T(8,128)} async-done(((f32[96,512]{1,0:T(8,128)}), f32[3072,512]{1,0:T(8,128)}) %all-gather.7.cloned.1.call-update) | async-done | bytes 6291472 | tf_op jit(solution)/shard_map/all_gather | solution.py:41
  311.8 2.3 dynamic-slice_select_fusion
  314.1 50.7 %all-gather.9.cloned.1.call-done = f32[4096,512]{1,0:T(8,128)} async-done(((f32[512,512]{1,0:T(8,128)}), f32[4096,512]{1,0:T(8,128)}) %all-gather.9.cloned.1.call-update) | async-done | bytes 8388624 | tf_op jit(solution)/shard_map/all_gather | solution.py:9
  364.7 4.5 %reduce_sum.9 = f32[512,512]{1,0:T(8,128)S(1)} reduce(f32[8,512,512]{2,1,0:T(8,128)} %bitcast.53, f32[]{:T(128)} %constant.175.clone.1), dimensions={0}, to_apply=%region_8.9 | reduce | flops 1835008 | bytes 9437188 | tf_op jit(solution)/shard_map/reduce_sum | solution.py:9
  369.2 14.9 %convolution_subtract_fusion = f32[3072,512]{1,0:T(8,128)} fusion(f32[3072,512]{1,0:T(8,128)} %param.4, f32[3072,512]{1,0:T(8,128)} %all-gather.7.cloned.1.call-done, f32[512,512]{1,0:T(8,128)S(1)} %reduce_sum.9), kind=kOutput, calls=%fused_computation.2 | convolution fusion | flops 9665249280 | bytes 19922944 | tf_op jit(solution)/shard_map/dot_general | solution.py:47
  (45 shorter events, 9.7 us)
Async XLA Ops:
  7.2 81.6 %all-gather.5.cloned.1.call-start = ((), (), s32[]{:S(2)}) async-start(), calls=%async_computation | async-start | bytes 1081344 | tf_op jit(solution)/shard_map/all_gather | solution.py:37
  7.9 303.9 %all-gather.7.cloned.1.call-start = ((), (), s32[]{:S(2)}) async-start(), calls=%async_computation.1 | async-start | bytes 6488064 | tf_op jit(solution)/shard_map/all_gather | solution.py:41
  225.5 139.2 %all-gather.9.cloned.1.call-start = ((), (), s32[]{:S(2)}) async-start(), calls=%async_computation.2 | async-start | bytes 9437184 | tf_op jit(solution)/shard_map/all_gather | solution.py:9
Sparse Core Ops, SparseCore 0:
  10.6 78.1 all-gather.4
  225.7 86.0 all-gather.6
  314.2 50.4 all-gather.8
